TPU v7x, 512 devices: a whole 4x4x16 slice. The times are simulated.
512 devices in a mesh: gr: 16 (over z_hi, y, core), gc: 32 (over x, z_lo).
Axes of the slice: x: 4, y: 4, z: 16 (z_hi: 2, z_lo: 8; z = z_hi * 8 + z_lo), core: 2. Of those that a mesh axis runs over, the one named last changes fastest.
Arguments:
- features: bfloat16 [65536, 1024], P(('gr', 'gc')), may hold values from -6 to 6
- weight: bfloat16 [1024, 1024], replicated, may hold values from -0.1875 to 0.1875
- cotangent: bfloat16 [65536, 1024], P(('gr', 'gc')), may hold values from -6 to 6
- block_values: bfloat16 [512, 16, 128, 128], P(('gr', 'gc')), as said below
- block_codes: int32 [512, 16], P(('gr', 'gc')), may hold values from 0 to 511, as said below
- block_count: int32 [512], P(('gr', 'gc')), may hold values from 1 to 16, as said below
Outputs:
- output: float32 [65536, 1024], P(('gr', 'gc'))
- input_grad: float32 [65536, 1024], P(('gr', 'gc'))
- weight_grad: float32 [1024, 1024], P('gc')
Inputs may be any that keep to these rules, and one draw needn't show every extreme that they name: `block_codes`: write code = row * 512 + column. In every slot, row lies in 0 to 0 and column is a block of a slice s + j * 32 with |j| <= 8 (same grid column, at most 8 grid rows away). The codes of the live slots of one slice differ from one another. Every diagonal block (block row equal to block column) is live. The live slots of a slice are its first block_count slots; the entries of later slots are not part of the adjacency. In every draw some slice has all 16 slots live. `block_values`: the adjacency is symmetric: a block is live exactly when its mirror block is, and its entries are the transpose of the mirror's.
All inputs are finite; a program needn't handle non-finite values.
Results may differ from a plain program's by a relative error of at most 0.0045.
Values may be sent and summed in bfloat16 or wider, within the bound.
No kernel may reach another device: no remote copies, remote signals or barrier semaphores. Data moves between devices by JAX's collectives and lax.ppermute only.
A program may use at most 64 MiB of HBM per device.

v0:
```python
import jax
import jax.numpy as jnp
from jax import lax
from jax.sharding import PartitionSpec as P


def dense_tile(row_index, block_index, active, values, piece_blocks, row_blocks):
    block_size = values.shape[-1]
    select_col = (block_index[:, None] == jnp.arange(piece_blocks)[None, :]) & active[:, None]
    select_row = row_index[:, None] == jnp.arange(row_blocks)[None, :]
    tiled = jnp.einsum(
        "ka,km,kij->aimj",
        select_row.astype(jnp.bfloat16),
        select_col.astype(jnp.bfloat16),
        values,
        preferred_element_type=jnp.float32,
    )
    return tiled.astype(jnp.bfloat16).reshape(row_blocks * block_size, piece_blocks * block_size)


def aggregate(source, layout):
    row_index, block_index, active, values = layout
    node_rows = source.shape[0]
    block_size = values.shape[-1]
    row_blocks = node_rows // block_size
    portion = lax.all_gather(source, "gr", axis=0, tiled=True)
    tile = dense_tile(
        row_index, block_index, active, values, portion.shape[0] // block_size, row_blocks
    )
    return jnp.dot(tile, portion, preferred_element_type=jnp.float32)


def local(features, weight, cotangent, block_values, block_codes, block_count):
    node_rows = features.shape[0]
    block_size = block_values.shape[-1]
    row_blocks = node_rows // block_size
    grid_cols = lax.axis_size("gc")
    grid_rows = lax.axis_size("gr")
    all_blocks = row_blocks * grid_rows * grid_cols
    slot_codes = block_codes[0]
    row_index = slot_codes // all_blocks
    column_block = slot_codes % all_blocks
    block_index = column_block // row_blocks // grid_cols * row_blocks + column_block % row_blocks
    active = jnp.arange(slot_codes.shape[0]) < block_count[0]
    layout = (row_index, block_index, active, block_values[0])
    projected = jnp.dot(features, weight, preferred_element_type=jnp.float32).astype(jnp.bfloat16)
    summed = aggregate(projected, layout)
    sigmoid = jax.nn.sigmoid(summed)
    output = summed * sigmoid
    act_slope = (cotangent.astype(jnp.float32) * sigmoid * (1.0 + summed * (1.0 - sigmoid))).astype(
        jnp.bfloat16
    )
    back_grad = aggregate(act_slope, layout).astype(jnp.bfloat16)
    input_grad = lax.dot_general(
        back_grad, weight, (((1,), (1,)), ((), ())), preferred_element_type=jnp.float32
    )
    grad_scale = (node_rows * grid_rows * grid_cols) ** (-0.5)
    partial_grad = (
        lax.dot_general(
            features, back_grad, (((0,), (0,)), ((), ())), preferred_element_type=jnp.float32
        )
        * grad_scale
    )
    row_share = lax.psum_scatter(partial_grad, "gc", scatter_dimension=0, tiled=True)
    weight_grad = lax.psum(row_share, "gr")
    return (output, input_grad, weight_grad)


def solution(mesh):
    in_specs = (
        P(("gr", "gc"), None),
        P(),
        P(("gr", "gc"), None),
        P(("gr", "gc"), None, None, None),
        P(("gr", "gc"), None),
        P(("gr", "gc")),
    )
    out_specs = (P(("gr", "gc"), None), P(("gr", "gc"), None), P("gc", None))
    return jax.shard_map(local, mesh=mesh, in_specs=in_specs, out_specs=out_specs, check_vma=False)
```

profile of v0, /device:TPU:1, one launch (start us, length us, event | category | flops | bytes accessed | tf_op | source)
XLA Modules:
  0.0 770.5 jit_solution(15007061973408233624)
XLA Ops:
  7.2 0.0 copy-start
  7.2 0.0 all-gather.3.cloned.1.call-start
  7.2 1.5 copy-done
  8.8 2.1 convolution_convert_fusion.1
  10.9 0.0 all-gather.3.cloned.1.call-update
  10.9 0.0 all-gather.5.cloned.1.call-start
  11.6 0.7 and_select_fusion.1
  12.3 0.7 compare_convert_fusion
  12.9 1.5 convolution_convert_fusion
  14.4 122.6 %all-gather.3.cloned.1.call-done = bf16[2048,1024]{1,0:T(8,128)(2,1)} async-done(((bf16[128,1024]{1,0:T(8,128)(2,1)}), bf16[2048,1024]{1,0:T(8,128)(2,1)}) %all-gather.3.cloned.1.call-update) | async-done | bytes 4194320 | tf_op jit(solution)/shard_map/all_gather | solution.py:26
  137.0 4.0 multiply_convert_fusion
  141.0 0.0 copy-start.1
  141.0 0.0 all-gather.5.cloned.1.call-update
  141.0 0.0 reduce-scatter.4.cloned.1.call-start
  141.1 112.4 %all-gather.5.cloned.1.call-done = bf16[2048,1024]{1,0:T(8,128)(2,1)} async-done(((bf16[128,1024]{1,0:T(8,128)(2,1)}), bf16[2048,1024]{1,0:T(8,128)(2,1)}) %all-gather.5.cloned.1.call-update) | async-done | bytes 4194320 | tf_op jit(solution)/shard_map/all_gather | solution.py:26
  253.5 2.9 convolution_convert_fusion.2
  256.4 0.0 copy-done.1
  256.4 2.7 multiply_bitcast_fusion
  259.1 5.4 copy.13
  264.5 0.0 reduce-scatter.4.cloned.1.call-update
  264.5 0.0 all-reduce.2.cloned.1.call-start
  264.6 222.1 %reduce-scatter.4.cloned.1.call-done = f32[32,1024]{1,0:T(8,128)} async-done(((f32[1024,1024]{1,0:T(8,128)}), f32[32,1024]{1,0:T(8,128)}) %reduce-scatter.4.cloned.1.call-update) | async-done | bytes 131088
  486.6 1.9 copy.14
  488.5 0.0 all-reduce.2.cloned.1.call-update
  488.6 1.6 fusion.16
  490.2 271.9 %all-reduce.2.cloned.1.call-done = f32[32,1024]{0,1:T(8,128)} async-done(((f32[32,1024]{0,1:T(8,128)}), f32[32,1024]{0,1:T(8,128)}) %all-reduce.2.cloned.1.call-update) | async-done | bytes 131088 | tf_op jit(solution)/shard_map/psum | solution.py:65
  762.1 1.9 copy.12
Async XLA Ops:
  7.2 1.6 copy-start
  7.2 129.8 %all-gather.3.cloned.1.call-start = ((), (), s32[]{:S(2)}) async-start(), calls=%async_computation.1 | async-start | bytes 4456448 | tf_op jit(solution)/shard_map/all_gather | solution.py:26
  10.9 242.6 %all-gather.5.cloned.1.call-start = ((), (), s32[]{:S(2)}) async-start(), calls=%async_computation.2 | async-start | bytes 4456448 | tf_op jit(solution)/shard_map/all_gather | solution.py:26
  141.0 115.4 %copy-start.1 = (bf16[128,1024]{1,0:T(8,128)(2,1)S(1)}, bf16[128,1024]{1,0:T(8,128)(2,1)}, u32[]{:S(2)}) copy-start(bf16[128,1024]{1,0:T(8,128)(2,1)} %param.6) | copy-start | bytes 786436
  141.0 345.6 %reduce-scatter.4.cloned.1.call-start = ((), (), s32[]{:S(2)}) async-start(), calls=%async_computation.4 | async-start | bytes 4325376
  264.5 497.6 %all-reduce.2.cloned.1.call-start = ((), (), s32[]{:S(2)}) async-start(), calls=%async_computation.3 | async-start | bytes 1048576 | tf_op jit(solution)/shard_map/psum | solution.py:65
Sparse Core Ops, SparseCore 0:
  11.9 125.0 all-gather.2
  141.1 112.3 all-gather.4
  264.6 221.9 reduce-scatter.3
  489.4 272.6 all-reduce.1
where the time goes:
time: 771 us; the launch traced here: 770 us
  waiting for transfers between devices  729 us (95%)
  matrix products  14.8 us (2%)
  between operations  14.4 us (2%)
  local copies, waits for them, and re-layouts  10.7 us (1%)
    psum x1, waiting for transfers between devices, local(): weight_grad = lax.psum(row_share, 'gr')  272 us
    all_gather x2, waiting for transfers between devices, aggregate(): portion = lax.all_gather(source, 'gr', axis=0, tiled=True)  235 us
    unnamed x5, waiting for transfers between devices  222 us
  transfers between devices with their start and end apart: 4, of which 4 were waited for; matrix products, arithmetic and copies ran while one was open for 1% of the time, Pallas kernels for 0%

commit v1 on v0

--- a/solution.py
+++ b/solution.py
@@ -62,7 +62,7 @@
         * grad_scale
     )
     row_share = lax.psum_scatter(partial_grad, "gc", scatter_dimension=0, tiled=True)
-    weight_grad = lax.psum(row_share, "gr")
+    weight_grad = jnp.sum(lax.all_gather(row_share, "gr"), axis=0)
     return (output, input_grad, weight_grad)
 
 

time: 771 us -> 608 us (0.79)
  waiting for transfers between devices: 729 us -> 568 us
    psum x1 -> x0, waiting for transfers between devices: 272 us -> none  [local(): weight_grad = lax.psum(row_share, 'gr')]
    reduce_scatter x0 -> x1, waiting for transfers between devices: none -> 222 us  [local(): lax.psum_scatter(partial_grad, 'gc', scatter_dimension=0, tiled=True)]
    unnamed x5 -> x4, waiting for transfers between devices: 222 us -> 0.07 us
    all_gather x0 -> x1, waiting for transfers between devices: none -> 111 us  [local(): weight_grad = jnp.sum(lax.all_gather(row_share, 'gr'), axis=0)]
where the time goes in v1:
time: 608 us
  waiting for transfers between devices  568 us (93%)
  matrix products  14.8 us (2%)
  between operations  14.4 us (2%)
  local copies, waits for them, and re-layouts  6.9 us (1%)
    all_gather x2, waiting for transfers between devices, aggregate(): portion = lax.all_gather(source, 'gr', axis=0, tiled=True)  235 us
    reduce_scatter x1, waiting for transfers between devices, local(): lax.psum_scatter(partial_grad, 'gc', scatter_dimension=0, tiled=True)  222 us
    all_gather x1, waiting for transfers between devices, local(): weight_grad = jnp.sum(lax.all_gather(row_share, 'gr'), axis=0)  111 us
  transfers between devices with their start and end apart: 4, of which 4 were waited for; matrix products, arithmetic and copies ran while one was open for 1% of the time, Pallas kernels for 0%

profile of v1, /device:TPU:1, one launch (start us, length us, event | category | flops | bytes accessed | tf_op | source)
XLA Modules:
  0.0 608.0 jit_solution(6698389082501045366)
XLA Ops:
  7.2 0.0 copy-start
  7.2 0.0 all-gather.5.cloned.1.call-start
  7.2 1.5 copy-done
  8.8 2.1 convolution_convert_fusion.1
  10.9 0.0 all-gather.5.cloned.1.call-update
  10.9 0.0 all-gather.7.cloned.1.call-start
  11.6 0.7 and_select_fusion.1
  12.3 0.7 compare_convert_fusion
  12.9 1.5 convolution_convert_fusion
  14.4 122.6 %all-gather.5.cloned.1.call-done = bf16[2048,1024]{1,0:T(8,128)(2,1)} async-done(((bf16[128,1024]{1,0:T(8,128)(2,1)}), bf16[2048,1024]{1,0:T(8,128)(2,1)}) %all-gather.5.cloned.1.call-update) | async-done | bytes 4194320 | tf_op jit(solution)/shard_map/all_gather | solution.py:26
  137.0 4.0 multiply_convert_fusion
  141.0 0.0 copy-start.1
  141.0 0.0 all-gather.7.cloned.1.call-update
  141.0 0.0 reduce-scatter.4.cloned.1.call-start
  141.1 112.4 %all-gather.7.cloned.1.call-done = bf16[2048,1024]{1,0:T(8,128)(2,1)} async-done(((bf16[128,1024]{1,0:T(8,128)(2,1)}), bf16[2048,1024]{1,0:T(8,128)(2,1)}) %all-gather.7.cloned.1.call-update) | async-done | bytes 4194320 | tf_op jit(solution)/shard_map/all_gather | solution.py:26
  253.5 2.9 convolution_convert_fusion.2
  256.4 0.0 copy-done.1
  256.4 2.7 multiply_bitcast_fusion
  259.1 5.4 copy.14
  264.5 0.0 reduce-scatter.4.cloned.1.call-update
  264.5 0.0 all-gather.9.cloned.1.call-start
  264.6 222.1 %reduce-scatter.4.cloned.1.call-done = f32[32,1024]{1,0:T(8,128)} async-done(((f32[1024,1024]{1,0:T(8,128)}), f32[32,1024]{1,0:T(8,128)}) %reduce-scatter.4.cloned.1.call-update) | async-done | bytes 131088 | tf_op jit(solution)/shard_map/reduce_scatter | solution.py:64
  486.6 0.0 all-gather.9.cloned.1.call-update
  486.7 1.6 fusion.16
  488.3 110.8 %all-gather.9.cloned.1.call-done = f32[512,1024]{1,0:T(8,128)} async-done(((f32[32,1024]{1,0:T(8,128)}), f32[512,1024]{1,0:T(8,128)}) %all-gather.9.cloned.1.call-update) | async-done | bytes 2097168 | tf_op jit(solution)/shard_map/all_gather | solution.py:65
  599.1 2.4 reduce_sum.9
Async XLA Ops:
  7.2 1.6 copy-start
  7.2 129.8 %all-gather.5.cloned.1.call-start = ((), (), s32[]{:S(2)}) async-start(), calls=%async_computation.1 | async-start | bytes 4456448 | tf_op jit(solution)/shard_map/all_gather | solution.py:26
  10.9 242.6 %all-gather.7.cloned.1.call-start = ((), (), s32[]{:S(2)}) async-start(), calls=%async_computation.2 | async-start | bytes 4456448 | tf_op jit(solution)/shard_map/all_gather | solution.py:26
  141.0 115.4 %copy-start.1 = (bf16[128,1024]{1,0:T(8,128)(2,1)S(1)}, bf16[128,1024]{1,0:T(8,128)(2,1)}, u32[]{:S(2)}) copy-start(bf16[128,1024]{1,0:T(8,128)(2,1)} %param.6) | copy-start | bytes 786436
  141.0 345.6 %reduce-scatter.4.cloned.1.call-start = ((), (), s32[]{:S(2)}) async-start(), calls=%async_computation.4 | async-start | bytes 4325376 | tf_op jit(solution)/shard_map/reduce_scatter | solution.py:64
  264.5 334.6 %all-gather.9.cloned.1.call-start = ((), (), s32[]{:S(2)}) async-start(), calls=%async_computation.3 | async-start | bytes 2228224 | tf_op jit(solution)/shard_map/all_gather | solution.py:65
Sparse Core Ops, SparseCore 0:
  11.9 125.0 all-gather.4
  141.1 112.3 all-gather.6
  264.6 221.9 reduce-scatter.3
  489.8 109.2 all-gather.8

commit v2 on v0

--- a/solution.py
+++ b/solution.py
@@ -23,7 +23,9 @@
     node_rows = source.shape[0]
     block_size = values.shape[-1]
     row_blocks = node_rows // block_size
-    portion = lax.all_gather(source, "gr", axis=0, tiled=True)
+    portion = jnp.concatenate(
+        lax.all_to_all(jnp.stack([source] * lax.axis_size("gr")), "gr", 0, 0), axis=0
+    )
     tile = dense_tile(
         row_index, block_index, active, values, portion.shape[0] // block_size, row_blocks
     )

time: 771 us -> 952 us (1.23)
  blocking collectives: 0 us -> 140 us
  waiting for transfers between devices: 729 us -> 753 us
  starting transfers between devices: 0.16 us -> 19.4 us
    all_gather x2 -> x0, waiting for transfers between devices: 235 us -> none  [aggregate(): portion = lax.all_gather(source, 'gr', axis=0, tiled=True)]
    unnamed x5 -> x3, waiting for transfers between devices: 222 us -> 387 us
    all_to_all x0 -> x1, blocking collectives: none -> 140 us  [aggregate(): lax.all_to_all(jnp.stack([source] * lax.axis_size('gr')), 'gr', 0, 0)]
    all_to_all x0 -> x1, waiting for transfers between devices: none -> 95.1 us  [aggregate(): lax.all_to_all(jnp.stack([source] * lax.axis_size('gr')), 'gr', 0, 0)]
    all_to_all x0 -> x1, starting transfers between devices: none -> 19.4 us  [aggregate(): lax.all_to_all(jnp.stack([source] * lax.axis_size('gr')), 'gr', 0, 0)]
  transfers between devices with their start and end apart: 4 -> 3, of which waited for: 4 -> 3; matrix products, arithmetic and copies ran while one was open for 1% -> 0% of each run, Pallas kernels for 0% -> 0%
where the time goes in v2:
time: 952 us
  waiting for transfers between devices  753 us (79%)
  blocking collectives  140 us (15%)
  starting transfers between devices  19.4 us (2%)
  between operations  14.8 us (2%)
  local copies, waits for them, and re-layouts  14 us (1%)
  matrix products  10.8 us (1%)
    unnamed x3, waiting for transfers between devices  387 us
    psum x1, waiting for transfers between devices, local(): weight_grad = lax.psum(row_share, 'gr')  271 us
    all_to_all x1, blocking collectives, aggregate(): lax.all_to_all(jnp.stack([source] * lax.axis_size('gr')), 'gr', 0, 0)  140 us
    all_to_all x1, waiting for transfers between devices, aggregate(): lax.all_to_all(jnp.stack([source] * lax.axis_size('gr')), 'gr', 0, 0)  95.1 us
    all_to_all x1, starting transfers between devices, aggregate(): lax.all_to_all(jnp.stack([source] * lax.axis_size('gr')), 'gr', 0, 0)  19.4 us
  transfers between devices with their start and end apart: 3, of which 3 were waited for; matrix products, arithmetic and copies ran while one was open for 0% of the time, Pallas kernels for 0%

profile of v2, /device:TPU:1, one launch (start us, length us, event | category | flops | bytes accessed | tf_op | source)
XLA Modules:
  0.0 951.7 jit_solution(14132679531708192601)
XLA Ops:
  7.2 0.0 copy-start
  7.2 1.6 copy-done
  8.8 1.4 convolution_convert_fusion.1
  10.2 2.5 stack.4
  12.7 0.0 copy-start.3
  12.7 0.0 copy-start.2
  12.7 0.0 copy-start.4
  12.7 19.4 %all-to-all-start = ((bf16[16,128,1024]{2,1,0:T(8,128)(2,1)}), bf16[16,128,1024]{2,1,0:T(8,128)(2,1)}, u32[]{:S(2)}, u32[]{:S(2)}) async-start(bf16[16,128,1024]{2,1,0:T(8,128)(2,1)} %stack.4), calls=%async_computation | async-start | bytes 8388608 | tf_op jit(solution)/shard_map/all_to_all | solution.py:27
  32.0 0.0 reduce-scatter.4.cloned.1.call-start
  32.7 0.0 copy-done.3
  32.8 0.0 copy-done.2
  32.8 0.4 convolution_convert_fusion
  33.2 95.1 %all-to-all-done = bf16[16,128,1024]{2,1,0:T(8,128)(2,1)} async-done(((bf16[16,128,1024]{2,1,0:T(8,128)(2,1)}), bf16[16,128,1024]{2,1,0:T(8,128)(2,1)}, u32[]{:S(2)}, u32[]{:S(2)}) %all-to-all-start) | async-done | bytes 4194336 | tf_op jit(solution)/shard_map/all_to_all | solution.py:27
  128.3 0.0 copy-done.4
  128.3 3.9 multiply_convert_fusion
  132.2 0.5 stack.5
  132.7 139.6 %all_to_all.10 = bf16[16,128,1024]{2,1,0:T(8,128)(2,1)S(1)} all-to-all(bf16[16,128,1024]{2,1,0:T(8,128)(2,1)S(1)} %stack.5), channel_id=1, replica_groups=mesh['gr'=16,'gc'=32] {'gr'}, dimensions={0} | all-to-all | bytes 8388608 | tf_op jit(solution)/shard_map/all_to_all | solution.py:27
  272.3 0.0 copy-start.1
  272.3 0.7 convolution_convert_fusion.2
  273.1 0.2 copy-done.1
  273.3 2.7 multiply_bitcast_fusion
  276.0 5.4 copy.13
  281.3 0.0 reduce-scatter.4.cloned.1.call-update
  281.4 0.0 all-reduce.2.cloned.1.call-start
  281.4 386.5 %reduce-scatter.4.cloned.1.call-done = f32[32,1024]{1,0:T(8,128)} async-done(((f32[1024,1024]{1,0:T(8,128)}), f32[32,1024]{1,0:T(8,128)}) %reduce-scatter.4.cloned.1.call-update) | async-done | bytes 131088
  667.9 1.9 copy.14
  669.9 0.0 all-reduce.2.cloned.1.call-update
  669.9 1.6 fusion.16
  671.5 271.5 %all-reduce.2.cloned.1.call-done = f32[32,1024]{0,1:T(8,128)} async-done(((f32[32,1024]{0,1:T(8,128)}), f32[32,1024]{0,1:T(8,128)}) %all-reduce.2.cloned.1.call-update) | async-done | bytes 131088 | tf_op jit(solution)/shard_map/psum | solution.py:67
  943.0 1.9 copy.12
  (2 shorter events, 0.0 us)
Async XLA Ops:
  7.2 1.6 copy-start
  12.7 20.1 %copy-start.3 = (s32[1,16]{1,0:T(1,128)S(1)}, s32[1,16]{1,0:T(1,128)}, u32[]{:S(2)}) copy-start(s32[1,16]{1,0:T(1,128)} %param.10) | copy-start | bytes 196
  12.7 20.1 %copy-start.2 = (bf16[1,16,128,128]{3,2,1,0:T(8,128)(2,1)S(1)}, bf16[1,16,128,128]{3,2,1,0:T(8,128)(2,1)}, u32[]{:S(2)}) copy-start(bf16[1,16,128,128]{3,2,1,0:T(8,128)(2,1)} %param.9) | copy-start | bytes 1572868
  12.7 115.6 %copy-start.4 = (bf16[128,1024]{1,0:T(8,128)(2,1)S(1)}, bf16[128,1024]{1,0:T(8,128)(2,1)}, u32[]{:S(2)}) copy-start(bf16[128,1024]{1,0:T(8,128)(2,1)} %param.8) | copy-start | bytes 786436
  12.7 115.6 %all-to-all-start = ((bf16[16,128,1024]{2,1,0:T(8,128)(2,1)}), bf16[16,128,1024]{2,1,0:T(8,128)(2,1)}, u32[]{:S(2)}, u32[]{:S(2)}) async-start(bf16[16,128,1024]{2,1,0:T(8,128)(2,1)} %stack.4), calls=%async_computation | async-start | bytes 8388608 | tf_op jit(solution)/shard_map/all_to_all | solution.py:27
  32.0 635.9 %reduce-scatter.4.cloned.1.call-start = ((), (), s32[]{:S(2)}) async-start(), calls=%async_computation.4 | async-start | bytes 4325376
  272.3 1.0 copy-start.1
  281.4 661.6 %all-reduce.2.cloned.1.call-start = ((), (), s32[]{:S(2)}) async-start(), calls=%async_computation.3 | async-start | bytes 1048576 | tf_op jit(solution)/shard_map/psum | solution.py:67
Sparse Core Ops, SparseCore 0:
  281.5 386.4 reduce-scatter.3
  670.8 272.0 all-reduce.1
